TPU v7x, 32 devices: a whole 2x2x4 slice. The times are simulated.
32 devices in a mesh: dp: 8 (over y, x, core), tensor: 4 (over z).
Axes of the slice: x: 2, y: 2, z: 4, core: 2. Of those that a mesh axis runs over, the one named last changes fastest.
Arguments:
- tokens: bfloat16 [8192, 2048], P(('dp', 'tensor')), may hold values from -6 to 6
- lengths: int32 [8], P('dp'), may hold values from 513 to 1024, as said below
- routes: int32 [8192, 4], P('dp'), may hold values from 0 to 7, all different within a row; in each aligned block of 1024 rows (0 to 1023, 1024 to 2047, ...) at most 768 rows name the same one
- cotangent: bfloat16 [8192, 2048], P(('dp', 'tensor')), may hold values from -6 to 6
- norm_one: bfloat16 [2048], replicated, may hold values from 0.5 to 1.5
- qkv_weight: bfloat16 [2048, 3, 2048], P(None, None, 'tensor'), may hold values from -0.125 to 0.125
- qkv_bias: bfloat16 [3, 2048], P(None, 'tensor'), may hold values from -0.59765625 to 0.59765625
- out_weight: bfloat16 [2048, 2048], P('tensor'), may hold values from -1.5 to 1.5
- norm_two: bfloat16 [2048], replicated, may hold values from 0.5 to 1.5
- router_weight: bfloat16 [2048, 8], replicated, may hold values from -0.0625 to 0.0625
- expert_in: bfloat16 [8, 2048, 2, 1408], P(None, None, None, 'tensor'), may hold values from -0.125 to 0.125
- expert_out: bfloat16 [8, 1408, 2048], P(None, 'tensor'), may hold values from -0.625 to 0.625
- shared_in: bfloat16 [2048, 2, 5632], P(None, None, 'tensor'), may hold values from -0.125 to 0.125
- shared_out: bfloat16 [5632, 2048], P('tensor'), may hold values from -0.15625 to 0.15625
- shared_gate: bfloat16 [2048], replicated, may hold values from -0.125 to 0.125
Outputs:
- output: bfloat16 [8192, 2048], P(('dp', 'tensor'))
- input_grad: float32 [8192, 2048], P(('dp', 'tensor'))
- norm_one_grad: float32 [2048], replicated
- qkv_weight_grad: float32 [2048, 3, 2048], P('dp', None, 'tensor')
- qkv_bias_grad: float32 [3, 2048], P(None, 'tensor')
- out_weight_grad: float32 [2048, 2048], P('tensor', 'dp')
- norm_two_grad: float32 [2048], replicated
- router_grad: float32 [2048, 8], replicated
- expert_in_grad: float32 [8, 2048, 2, 1408], P(None, 'dp', None, 'tensor')
- expert_out_grad: float32 [8, 1408, 2048], P(None, 'tensor', 'dp')
- shared_in_grad: float32 [2048, 2, 5632], P('dp', None, 'tensor')
- shared_out_grad: float32 [5632, 2048], P('tensor', 'dp')
- shared_gate_grad: float32 [2048], replicated
Inputs may be any that keep to these rules, and one draw needn't show every extreme that they name: Row r holds one sequence in its first lengths[r] slots; the other slots are padding. In every draw some row is full. `routes`: the 4 experts of a slot are all different. Within each packed row (aligned blocks of 1024 slots) no expert is named more than 768 times; in some row some expert is named exactly 768 times.
All inputs are finite; a program needn't handle non-finite values.
Results may differ from a plain program's by a relative error of at most 0.018.
The roundings to bfloat16 on the way count: a program that leaves them out, or rounds other values in their place, can miss the bound.
Values may be sent and summed in bfloat16 or wider, within the bound.
A program may use at most 384 MiB of HBM per device.

v0:
```python
import jax
import jax.numpy as jnp
from jax import lax
from jax.sharding import PartitionSpec as P

HEAD_DIM = 128
epsilon = 1e-06
theta_base = 1000000.0
precise = lax.Precision.HIGHEST


def rotary_tables(row_count, head_width):
    half_index = jnp.arange(head_width // 2).astype(jnp.float32)
    frequency = theta_base ** (-2.0 * half_index / head_width)
    angles = jnp.arange(row_count).astype(jnp.float32)[:, None] * frequency[None, :]
    angles = jnp.concatenate([angles, angles], axis=-1)
    return (jnp.cos(angles)[:, None, :], jnp.sin(angles)[:, None, :])


def rotary(values, cos_table, sine_table):
    half_width = values.shape[-1] // 2
    turned = jnp.concatenate([-values[..., half_width:], values[..., :half_width]], axis=-1)
    return values * cos_table + turned * sine_table


def rotary_back(grads_in, cos_table, sine_table):
    half_width = grads_in.shape[-1] // 2
    scaled = grads_in * sine_table
    return grads_in * cos_table + jnp.concatenate(
        [scaled[..., half_width:], -scaled[..., :half_width]], axis=-1
    )


def swiglu_back(gate_up, d_inner):
    gate_part = gate_up[:, 0]
    up_part = gate_up[:, 1]
    gate_sig = jax.nn.sigmoid(gate_part)
    d_gate = d_inner * up_part * gate_sig * (1.0 + gate_part * (1.0 - gate_sig))
    d_up = d_inner * gate_part * gate_sig
    return jnp.stack([d_gate, d_up], axis=1)


def norm_back(d_normed, unit_rows, inverse, gain_vector):
    d_unit = d_normed * gain_vector
    return inverse * (d_unit - unit_rows * jnp.mean(d_unit * unit_rows, axis=-1, keepdims=True))


def expert_forward(row_data, in_weight, down_weight):
    in_flat = in_weight.reshape(in_weight.shape[0], -1)
    gate_up = jnp.dot(row_data, in_flat, preferred_element_type=jnp.float32).reshape(
        row_data.shape[0], 2, -1
    )
    inner_act = (jax.nn.silu(gate_up[:, 0]) * gate_up[:, 1]).astype(jnp.bfloat16)
    result = jnp.dot(inner_act, down_weight, preferred_element_type=jnp.float32)
    return (gate_up, inner_act, result)


def expert_backward(row_data, d_rows, scale_rows, gate_up, inner_act, in_weight, down_weight):
    d_result = (scale_rows[:, None] * d_rows).astype(jnp.bfloat16)
    down_grad = jnp.einsum("nf,nd->fd", inner_act, d_result, preferred_element_type=jnp.float32)
    d_inner = jnp.einsum("nd,fd->nf", d_result, down_weight, preferred_element_type=jnp.float32)
    projected = jnp.einsum("nd,fd->nf", d_rows, down_weight, preferred_element_type=jnp.float32)
    d_scale = jnp.sum(projected * inner_act.astype(jnp.float32), axis=-1)
    d_gate_up = swiglu_back(gate_up, d_inner).reshape(row_data.shape[0], -1).astype(jnp.bfloat16)
    in_flat = in_weight.reshape(in_weight.shape[0], -1)
    in_grad = jnp.einsum("nd,nc->dc", row_data, d_gate_up, preferred_element_type=jnp.float32)
    d_rows_in = jnp.einsum("nc,dc->nd", d_gate_up, in_flat, preferred_element_type=jnp.float32)
    return (in_grad.reshape(in_weight.shape), down_grad, d_scale, d_rows_in)


def on_device(
    tokens,
    lengths,
    routes,
    cotangent,
    norm_one,
    qkv_weight,
    qkv_bias,
    out_weight,
    norm_two,
    router_weight,
    expert_in,
    expert_out,
    shared_in,
    shared_out,
    shared_gate,
):
    own_rows = tokens.shape[0]
    slot_count = routes.shape[0]
    model_width = tokens.shape[1]
    qkv_cols = qkv_weight.shape[2]
    local_heads = qkv_cols // HEAD_DIM
    experts_total = router_weight.shape[1]
    length = lengths[0]
    tensor_index = lax.axis_index("tensor")
    first_row = tensor_index * own_rows
    slot_index = jnp.arange(slot_count)
    live_own = (first_row + jnp.arange(own_rows) < length).astype(jnp.float32)[:, None]
    block_rows = min(512, slot_count)
    scale = HEAD_DIM ** (-0.5)
    tokens_f = tokens.astype(jnp.float32)
    gain_one = norm_one.astype(jnp.float32)
    gain_two = norm_two.astype(jnp.float32)
    inv_one = lax.rsqrt(jnp.mean(tokens_f * tokens_f, axis=-1, keepdims=True) + epsilon)
    unit_one = tokens_f * inv_one
    normed_one = lax.all_gather(
        (unit_one * gain_one).astype(jnp.bfloat16), "tensor", axis=0, tiled=True
    )
    qkv_flat_weight = qkv_weight.reshape(model_width, 3 * qkv_cols)
    qkv_all = jnp.dot(normed_one, qkv_flat_weight, preferred_element_type=jnp.float32)
    qkv_all = qkv_all.reshape(slot_count, 3, qkv_cols) + qkv_bias.astype(jnp.float32)
    cos_table, sine_table = rotary_tables(slot_count, HEAD_DIM)
    query_heads = rotary(
        qkv_all[:, 0].reshape(slot_count, local_heads, HEAD_DIM), cos_table, sine_table
    ).astype(jnp.bfloat16)
    key_heads = rotary(
        qkv_all[:, 1].reshape(slot_count, local_heads, HEAD_DIM), cos_table, sine_table
    ).astype(jnp.bfloat16)
    value_heads = qkv_all[:, 2].reshape(slot_count, local_heads, HEAD_DIM).astype(jnp.bfloat16)

    def block_scores(block_start, block_end):
        raw_scores = (
            jnp.einsum(
                "qhd,khd->hqk",
                query_heads[block_start:block_end],
                key_heads[:block_end],
                preferred_element_type=jnp.float32,
            )
            * scale
        )
        allowed = (slot_index[None, :block_end] <= slot_index[block_start:block_end, None]) & (
            slot_index[None, :block_end] < length
        )
        return jnp.where(allowed[None], raw_scores, -1000000000.0)

    mixed_parts = []
    lse_parts = []
    for block_start in range(0, slot_count, block_rows):
        block_end = block_start + block_rows
        raw_scores = block_scores(block_start, block_end)
        row_peak = jnp.max(raw_scores, axis=-1, keepdims=True)
        exp_terms = jnp.exp(raw_scores - row_peak)
        summed = jnp.sum(exp_terms, axis=-1, keepdims=True)
        probs_low = (exp_terms / summed).astype(jnp.bfloat16)
        mixed_parts.append(
            jnp.einsum(
                "hqk,khd->qhd",
                probs_low,
                value_heads[:block_end],
                preferred_element_type=jnp.float32,
            )
        )
        lse_parts.append(row_peak + jnp.log(summed))
    mixed = jnp.concatenate(mixed_parts, axis=0).reshape(slot_count, qkv_cols).astype(jnp.bfloat16)
    branch_one = lax.psum_scatter(
        jnp.dot(mixed, out_weight, preferred_element_type=jnp.float32),
        "tensor",
        scatter_dimension=0,
        tiled=True,
    )
    hidden = tokens_f + live_own * branch_one
    inv_two = lax.rsqrt(jnp.mean(hidden * hidden, axis=-1, keepdims=True) + epsilon)
    unit_two = hidden * inv_two
    normed_two = lax.all_gather(
        (unit_two * gain_two).astype(jnp.bfloat16), "tensor", axis=0, tiled=True
    )
    router_probs = jax.nn.softmax(
        jnp.dot(normed_two, router_weight, preferred_element_type=jnp.float32), axis=-1
    )
    picked = jnp.sum(
        (routes[:, :, None] == jnp.arange(experts_total)[None, None, :]).astype(jnp.float32), axis=1
    )
    weights = router_probs * picked
    combined = jnp.zeros((slot_count, model_width), jnp.float32)
    kept_rows = []
    for expert in range(experts_total):
        gate_up, inner_act, result = expert_forward(
            normed_two, expert_in[expert], expert_out[expert]
        )
        combined = combined + weights[:, expert : expert + 1] * result
        kept_rows.append((gate_up, inner_act))
    shared_up, shared_act, shared_result = expert_forward(normed_two, shared_in, shared_out)
    gate_value = jax.nn.sigmoid(
        jnp.dot(normed_two, shared_gate, preferred_element_type=jnp.float32)
    )
    combined = combined + gate_value[:, None] * shared_result
    branch_two = lax.psum_scatter(
        combined.astype(jnp.bfloat16), "tensor", scatter_dimension=0, tiled=True
    ).astype(jnp.float32)
    output = (hidden + live_own * branch_two).astype(jnp.bfloat16)
    grad_out = cotangent.astype(jnp.float32) * live_own
    d_two = lax.all_gather((live_own * grad_out).astype(jnp.bfloat16), "tensor", axis=0, tiled=True)
    shared_in_grad, shared_out_grad, d_shared_scale, d_normed = expert_backward(
        normed_two, d_two, gate_value, shared_up, shared_act, shared_in, shared_out
    )
    d_gate_logit = d_shared_scale * gate_value * (1.0 - gate_value)
    in_grads = []
    out_grads = []
    d_columns = []
    for expert in range(experts_total):
        gate_up, inner_act = kept_rows[expert]
        in_grad, down_grad, d_scale, d_rows_in = expert_backward(
            normed_two,
            d_two,
            weights[:, expert],
            gate_up,
            inner_act,
            expert_in[expert],
            expert_out[expert],
        )
        d_normed = d_normed + d_rows_in
        d_columns.append(d_scale)
        in_grads.append(in_grad)
        out_grads.append(down_grad)
    expert_in_grad = jnp.stack(in_grads, axis=0)
    expert_out_grad = jnp.stack(out_grads, axis=0)
    d_probs = jnp.stack(d_columns, axis=1) * picked
    d_logits = router_probs * (d_probs - jnp.sum(router_probs * d_probs, axis=-1, keepdims=True))
    d_normed = d_normed + jnp.einsum(
        "se,de->sd", d_logits, router_weight.astype(jnp.float32), precision=precise
    )
    d_normed = d_normed + d_gate_logit[:, None] * shared_gate.astype(jnp.float32)[None, :]
    small_cols = jnp.concatenate([d_logits, d_gate_logit[:, None]], axis=1)
    col_sums = jnp.einsum(
        "sc,sd->cd", small_cols, normed_two.astype(jnp.float32), precision=precise
    )
    router_part = col_sums[:experts_total].T
    gate_part = col_sums[experts_total]
    grad_two = lax.psum_scatter(d_normed, "tensor", scatter_dimension=0, tiled=True)
    norm_two_part = jnp.sum(grad_two * unit_two, axis=0)
    grad_hidden = grad_out + norm_back(grad_two, unit_two, inv_two, gain_two)
    d_one = lax.all_gather(
        (live_own * grad_hidden).astype(jnp.bfloat16), "tensor", axis=0, tiled=True
    )
    out_weight_grad = jnp.einsum("sc,sd->cd", mixed, d_one, preferred_element_type=jnp.float32)
    d_mixed = jnp.einsum("sd,cd->sc", d_one, out_weight, preferred_element_type=jnp.float32)
    d_mixed = d_mixed.astype(jnp.bfloat16).reshape(slot_count, local_heads, HEAD_DIM)
    d_query_parts = []
    d_key = jnp.zeros((slot_count, local_heads, HEAD_DIM), jnp.float32)
    d_value = jnp.zeros((slot_count, local_heads, HEAD_DIM), jnp.float32)
    for block_number, block_start in enumerate(range(0, slot_count, block_rows)):
        block_end = block_start + block_rows
        raw_scores = block_scores(block_start, block_end)
        probs_full = jnp.exp(raw_scores - lse_parts[block_number])
        probs_low = probs_full.astype(jnp.bfloat16)
        d_grad_block = d_mixed[block_start:block_end]
        d_probs_att = jnp.einsum(
            "qhd,khd->hqk",
            d_grad_block,
            value_heads[:block_end],
            preferred_element_type=jnp.float32,
        )
        delta_sum = jnp.sum(probs_full * d_probs_att, axis=-1, keepdims=True)
        d_scores = (probs_full * (d_probs_att - delta_sum)).astype(jnp.bfloat16)
        d_query_parts.append(
            jnp.einsum(
                "hqk,khd->qhd", d_scores, key_heads[:block_end], preferred_element_type=jnp.float32
            )
            * scale
        )
        d_key = d_key.at[:block_end].add(
            jnp.einsum(
                "hqk,qhd->khd",
                d_scores,
                query_heads[block_start:block_end],
                preferred_element_type=jnp.float32,
            )
            * scale
        )
        d_value = d_value.at[:block_end].add(
            jnp.einsum("hqk,qhd->khd", probs_low, d_grad_block, preferred_element_type=jnp.float32)
        )
    d_query = jnp.concatenate(d_query_parts, axis=0)
    d_qkv = jnp.stack(
        [
            rotary_back(d_query, cos_table, sine_table).reshape(slot_count, qkv_cols),
            rotary_back(d_key, cos_table, sine_table).reshape(slot_count, qkv_cols),
            d_value.reshape(slot_count, qkv_cols),
        ],
        axis=1,
    ).astype(jnp.bfloat16)
    d_qkv_flat = d_qkv.reshape(slot_count, 3 * qkv_cols)
    qkv_weight_grad = jnp.einsum(
        "sd,sc->dc", normed_one, d_qkv_flat, preferred_element_type=jnp.float32
    )
    qkv_weight_grad = qkv_weight_grad.reshape(model_width, 3, qkv_cols)
    bias_part = jnp.sum(d_qkv.astype(jnp.float32), axis=0)
    grad_one = jnp.einsum(
        "sc,dc->sd", d_qkv_flat, qkv_flat_weight, preferred_element_type=jnp.float32
    )
    grad_one = lax.psum_scatter(
        grad_one.astype(jnp.bfloat16), "tensor", scatter_dimension=0, tiled=True
    ).astype(jnp.float32)
    norm_one_part = jnp.sum(grad_one * unit_one, axis=0)
    input_grad = grad_hidden + norm_back(grad_one, unit_one, inv_one, gain_one)
    column_start = tensor_index * qkv_cols
    zero_index = jnp.zeros((), jnp.int32)
    bias_full = lax.dynamic_update_slice(
        jnp.zeros((3, qkv_cols * lax.axis_size("tensor")), jnp.float32),
        bias_part,
        (zero_index, column_start),
    )
    norm_one_grad, norm_two_grad, router_grad, shared_gate_grad, bias_sum = lax.psum(
        (norm_one_part, norm_two_part, router_part, gate_part, bias_full), ("dp", "tensor")
    )
    qkv_bias_grad = lax.dynamic_slice(bias_sum, (zero_index, column_start), (3, qkv_cols))
    qkv_sum, out_sum, expert_in_sum, expert_out_sum, shared_in_sum, shared_out_sum = (
        lax.psum_scatter(
            qkv_weight_grad.astype(jnp.bfloat16), "dp", scatter_dimension=0, tiled=True
        ).astype(jnp.float32),
        lax.psum_scatter(
            out_weight_grad.astype(jnp.bfloat16), "dp", scatter_dimension=1, tiled=True
        ).astype(jnp.float32),
        lax.psum_scatter(
            expert_in_grad.astype(jnp.bfloat16), "dp", scatter_dimension=1, tiled=True
        ).astype(jnp.float32),
        lax.psum_scatter(
            expert_out_grad.astype(jnp.bfloat16), "dp", scatter_dimension=2, tiled=True
        ).astype(jnp.float32),
        lax.psum_scatter(
            shared_in_grad.astype(jnp.bfloat16), "dp", scatter_dimension=0, tiled=True
        ).astype(jnp.float32),
        lax.psum_scatter(
            shared_out_grad.astype(jnp.bfloat16), "dp", scatter_dimension=1, tiled=True
        ).astype(jnp.float32),
    )
    return (
        output,
        input_grad,
        norm_one_grad,
        qkv_sum,
        qkv_bias_grad,
        out_sum,
        norm_two_grad,
        router_grad,
        expert_in_sum,
        expert_out_sum,
        shared_in_sum,
        shared_out_sum,
        shared_gate_grad,
    )


def solution(mesh):
    in_specs = (
        P(("dp", "tensor"), None),
        P("dp"),
        P("dp", None),
        P(("dp", "tensor"), None),
        P(),
        P(None, None, "tensor"),
        P(None, "tensor"),
        P("tensor", None),
        P(),
        P(),
        P(None, None, None, "tensor"),
        P(None, "tensor", None),
        P(None, None, "tensor"),
        P("tensor", None),
        P(),
    )
    out_specs = (
        P(("dp", "tensor"), None),
        P(("dp", "tensor"), None),
        P(),
        P("dp", None, "tensor"),
        P(None, "tensor"),
        P("tensor", "dp"),
        P(),
        P(),
        P(None, "dp", None, "tensor"),
        P(None, "tensor", "dp"),
        P("dp", None, "tensor"),
        P("tensor", "dp"),
        P(),
    )
    return jax.shard_map(
        on_device, mesh=mesh, in_specs=in_specs, out_specs=out_specs, check_vma=False
    )
```

profile of v0, /device:TPU:1, one launch (start us, length us, event | category | flops | bytes accessed | tf_op | source)
XLA Modules:
  0.0 1673.9 jit_solution(9152987854078074397)
XLA Ops:
  26.3 69.4 %all-gather.5.cloned.1.call-done = bf16[1024,2048]{1,0:T(8,128)(2,1)} async-done(((bf16[256,2048]{1,0:T(8,128)(2,1)}), bf16[1024,2048]{1,0:T(8,128)(2,1)}) %all-gather.5.cloned.1.call-update) | async-done | bytes 4194320 | tf_op jit(solution)/shard_map/all_gather | solution.py:106
  140.0 142.3 %reduce-scatter.11.cloned.1.call-done = f32[256,2048]{1,0:T(8,128)} async-done(((f32[1024,2048]{1,0:T(8,128)}), f32[256,2048]{1,0:T(8,128)}) %reduce-scatter.11.cloned.1.call-update) | async-done | bytes 2097168 | tf_op jit(solution)/shard_map/reduce_scatter | solution.py:155
  289.6 11.4 copy.161
  301.1 15.1 copy.107
  316.8 16.4 fusion.447
  333.3 36.9 %all-gather.7.cloned.1.call-done = bf16[1024,2048]{1,0:T(8,128)(2,1)} async-done(((bf16[256,2048]{1,0:T(8,128)(2,1)}), bf16[1024,2048]{1,0:T(8,128)(2,1)}) %all-gather.7.cloned.1.call-update) | async-done | bytes 4194320 | tf_op jit(solution)/shard_map/all_gather | solution.py:164
  417.0 34.5 %all-gather.9.cloned.1.call-done = bf16[1024,2048]{1,0:T(8,128)(2,1)} async-done(((bf16[256,2048]{1,0:T(8,128)(2,1)}), bf16[1024,2048]{1,0:T(8,128)(2,1)}) %all-gather.9.cloned.1.call-update) | async-done | bytes 4194320 | tf_op jit(solution)/shard_map/all_gather | solution.py:192
  471.8 17.7 %fusion.46 = f32[1024,2,1408]{2,0,1:T(8,128)S(1)} fusion(bf16[2,1408,2048]{2,1,0:T(8,128)(2,1)} %bitcast.918, bf16[1024,2048]{1,0:T(8,128)(2,1)} %all-gather.7.cloned.1.call-done), kind=kOutput, calls=%fused_computation.74 | convolution fusion | flops 11811160064 | bytes 27262976 | tf_op jit(solution)/shard_map/dot_general | solution.py:50
  595.8 12.7 multiply_bitcast_fusion.1
  608.5 38.0 %fusion.19 = f32[1024,2048]{1,0:T(8,128)} fusion(f32[1024,2048]{1,0:T(8,128)} %fusion.501, f32[1024,2048]{1,0:T(8,128)} %fusion.500, f32[1024,2048]{1,0:T(8,128)} %fusion.499, f32[1024,2048]{1,0:T(8,128)} %fusion.498, f32[1024,2048]{1,0:T(8,128)} %fusion.497, f32[1024,2048]{1,0:T(8,128)} %fusion.496, f32[1024,2048]{1,0:T(8,128)} %fusion.495, ...), kind=kOutput, calls=%fused_computation.32 | convolution fusion | flops 11837112320 | bytes 101199872 | tf_op jit(solution)/shard_map/nc,dc->nd/dot_general | solution.py:67
  697.5 29.5 %add_convert_fusion = bf16[1024,2048]{1,0:T(8,128)(2,1)} fusion(f32[1024,2048]{1,0:T(8,128)} %fusion.319, f32[1024,2048]{1,0:T(8,128)} %fusion.323, f32[1024,2048]{1,0:T(8,128)} %fusion.327, f32[1024,2048]{1,0:T(8,128)} %fusion.331, f32[1024,2048]{1,0:T(8,128)} %fusion.335, f32[1024,2048]{1,0:T(8,128)} %fusion.339, f32[1024,2048]{1,0:T(8,128)} %fusion.343, ...), kind=kOutput, calls=%fused_computation.36 | convolution fusion | flops 5943328768 | bytes 79990784 | tf_op jit(solution)/shard_map/dot_general | solution.py:54
  727.1 62.4 %reduce-scatter.15.cloned.1.call-done = f32[256,2048]{1,0:T(8,128)} async-done(((f32[1024,2048]{1,0:T(8,128)}), f32[256,2048]{1,0:T(8,128)}) %reduce-scatter.15.cloned.1.call-update) | async-done | bytes 2097168 | tf_op jit(solution)/shard_map/reduce_scatter | solution.py:229
  792.9 77.0 %reduce-scatter.13.cloned.1.call-done = bf16[256,2048]{1,0:T(8,128)(2,1)} async-done(((bf16[1024,2048]{1,0:T(8,128)(2,1)}), bf16[256,2048]{1,0:T(8,128)(2,1)}) %reduce-scatter.13.cloned.1.call-update) | async-done | bytes 1048592 | tf_op jit(solution)/shard_map/reduce_scatter | solution.py:187
  875.8 10.7 convolution_convert_fusion.1
  928.6 19.2 %convolution_convert_fusion = bf16[2048,2,1408]{2,0,1:T(8,128)(2,1)} fusion(bf16[1024,2,1408]{0,2,1:T(8,128)(2,1)} %copy.137, bf16[1024,2048]{1,0:T(8,128)(2,1)} %all-gather.7.cloned.1.call-done), kind=kOutput, calls=%fused_computation.12 | convolution fusion | flops 11816927232 | bytes 21495808 | tf_op jit(solution)/shard_map/nd,nc->dc/dot_general | solution.py:66
  1028.5 12.0 bitcast_convert_fusion
  1045.3 11.5 convolution_convert_fusion.2
  1112.1 86.9 %reduce-scatter.27.cloned.1.call-done = bf16[256,2,1408]{2,0,1:T(8,128)(2,1)} async-done(((bf16[2048,2,1408]{2,0,1:T(8,128)(2,1)}), bf16[256,2,1408]{2,0,1:T(8,128)(2,1)}) %reduce-scatter.27.cloned.1.call-update) | async-done | bytes 1441808 | tf_op jit(solution)/shard_map/reduce_scatter | solution.py:320
  1203.5 40.1 %reduce-scatter.21.cloned.1.call-done = bf16[512,256]{1,0:T(8,128)(2,1)} async-done(((bf16[512,2048]{1,0:T(8,128)(2,1)}), bf16[512,256]{1,0:T(8,128)(2,1)}) %reduce-scatter.21.cloned.1.call-update) | async-done | bytes 262160 | tf_op jit(solution)/shard_map/reduce_scatter | solution.py:311
  1245.4 77.9 %reduce-scatter.17.cloned.1.call-done = bf16[256,2048]{1,0:T(8,128)(2,1)} async-done(((bf16[1024,2048]{1,0:T(8,128)(2,1)}), bf16[256,2048]{1,0:T(8,128)(2,1)}) %reduce-scatter.17.cloned.1.call-update) | async-done | bytes 1048592 | tf_op jit(solution)/shard_map/reduce_scatter | solution.py:291
  1325.4 42.1 %all-reduce.2 = (f32[2048]{0:T(1024)}, f32[3,2048]{1,0:T(4,128)S(1)}, f32[2048]{0:T(1024)}, f32[2048]{0:T(1024)}) all-reduce(f32[2048]{0:T(1024)S(1)} %get-tuple-element.118, f32[3,2048]{1,0:T(4,128)S(1)} %constant_dynamic-update-slice_fusion, f32[2048]{0:T(1024)S(1)} %copy-done.152, ...), channel_id=1, replica_groups=mesh['dp'=8,'tensor'=4] {'dp','tensor'}, use_global_device_ids=true, to_apply=%region_28.29 | all-reduce | flops 12288 | bytes 98304 | tf_op jit(solution)/shard_map/psum | solution.py:303
  1371.9 17.6 %reduce-scatter.19.cloned.1.call-done = bf16[256,3,512]{2,0,1:T(8,128)(2,1)} async-done(((bf16[2048,3,512]{2,0,1:T(8,128)(2,1)}), bf16[256,3,512]{2,0,1:T(8,128)(2,1)}) %reduce-scatter.19.cloned.1.call-update) | async-done | bytes 786448 | tf_op jit(solution)/shard_map/reduce_scatter | solution.py:308
  1392.0 147.4 %reduce-scatter.23.cloned.1.call-done = bf16[8,256,2,352]{1,3,2,0:T(8,128)(2,1)} async-done(((bf16[8,2048,2,352]{1,3,2,0:T(8,128)(2,1)}), bf16[8,256,2,352]{1,3,2,0:T(8,128)(2,1)}) %reduce-scatter.23.cloned.1.call-update) | async-done | bytes 2883600 | tf_op jit(solution)/shard_map/reduce_scatter | solution.py:314
  1544.4 121.3 %all-reduce.5.cloned.1.call-done = f32[2048,8]{0,1:T(8,128)} async-done(((f32[2048,8]{0,1:T(8,128)}), f32[2048,8]{0,1:T(8,128)}) %all-reduce.5.cloned.1.call-update) | async-done | bytes 65552 | tf_op jit(solution)/shard_map/psum | solution.py:303
  (604 shorter events, 506.5 us)
Async XLA Ops:
  7.2 88.5 %all-gather.5.cloned.1.call-start = ((), (), s32[]{:S(2)}) async-start(), calls=%async_computation.10 | async-start | bytes 5242880 | tf_op jit(solution)/shard_map/all_gather | solution.py:106
  12.7 269.6 %reduce-scatter.11.cloned.1.call-start = ((), (), s32[]{:S(2)}) async-start(), calls=%async_computation.11 | async-start | bytes 10485760 | tf_op jit(solution)/shard_map/reduce_scatter | solution.py:155
  139.3 143.0 %copy-start.10 = (bf16[256,2048]{1,0:T(8,128)(2,1)S(1)}, bf16[256,2048]{1,0:T(8,128)(2,1)}, u32[]{:S(2)}) copy-start(bf16[256,2048]{1,0:T(8,128)(2,1)} %param.27) | copy-start | bytes 3145732
  139.3 230.9 %all-gather.7.cloned.1.call-start = ((), (), s32[]{:S(2)}) async-start(), calls=%async_computation.12 | async-start | bytes 5242880 | tf_op jit(solution)/shard_map/all_gather | solution.py:164
  140.0 145.9 %copy-start.129 = (f32[2048]{0:T(1024)}, f32[2048]{0:T(1024)S(1)}, u32[]{:S(2)}) copy-start(f32[2048]{0:T(1024)S(1)} %convert_element_type.408) | copy-start | bytes 24580
  140.0 145.8 %copy-start.164 = (f32[256]{0:T(256)}, f32[256]{0:T(256)S(1)}, u32[]{:S(2)}) copy-start(f32[256]{0:T(256)S(1)} %compare_convert_fusion) | copy-start | bytes 3076
  288.4 163.2 %all-gather.9.cloned.1.call-start = ((), (), s32[]{:S(2)}) async-start(), calls=%async_computation.14 | async-start | bytes 5242880 | tf_op jit(solution)/shard_map/all_gather | solution.py:192
  333.2 456.3 %reduce-scatter.15.cloned.1.call-start = ((), (), s32[]{:S(2)}) async-start(), calls=%async_computation.15 | async-start | bytes 10485760 | tf_op jit(solution)/shard_map/reduce_scatter | solution.py:229
  646.5 223.4 %reduce-scatter.13.cloned.1.call-start = ((), (), s32[]{:S(2)}) async-start(), calls=%async_computation.13 | async-start | bytes 5242880 | tf_op jit(solution)/shard_map/reduce_scatter | solution.py:187
  727.0 142.9 %copy-start.28 = (bf16[256,2048]{1,0:T(8,128)(2,1)S(1)}, bf16[256,2048]{1,0:T(8,128)(2,1)}, u32[]{:S(2)}) copy-start(bf16[256,2048]{1,0:T(8,128)(2,1)} %param.30) | copy-start | bytes 3145732
  727.0 142.9 %copy-start.165 = (f32[256]{0:T(256)S(1)}, f32[256]{0:T(256)}, u32[]{:S(2)}) copy-start(f32[256]{0:T(256)} %copy-done.164) | copy-start | bytes 3076
  727.0 230.1 %all-gather.11.cloned.1.call-start = ((), (), s32[]{:S(2)}) async-start(), calls=%async_computation.16 | async-start | bytes 5242880 | tf_op jit(solution)/shard_map/all_gather | solution.py:232
  875.8 226.7 %reduce-scatter.29.cloned.1.call-start = ((), (), s32[]{:S(2)}) async-start(), calls=%async_computation.24 | async-start | bytes 6488064 | tf_op jit(solution)/shard_map/reduce_scatter | solution.py:323
  886.6 222.3 %reduce-scatter.25.cloned.1.call-start = ((), (), s32[]{:S(2)}) async-start(), calls=%async_computation.22 | async-start | bytes 12976128 | tf_op jit(solution)/shard_map/reduce_scatter | solution.py:317
  913.9 285.2 %reduce-scatter.27.cloned.1.call-start = ((), (), s32[]{:S(2)}) async-start(), calls=%async_computation.23 | async-start | bytes 12976128 | tf_op jit(solution)/shard_map/reduce_scatter | solution.py:320
  947.8 295.8 %reduce-scatter.21.cloned.1.call-start = ((), (), s32[]{:S(2)}) async-start(), calls=%async_computation.19 | async-start | bytes 2359296 | tf_op jit(solution)/shard_map/reduce_scatter | solution.py:311
  989.0 334.3 %reduce-scatter.17.cloned.1.call-start = ((), (), s32[]{:S(2)}) async-start(), calls=%async_computation.17 | async-start | bytes 5242880 | tf_op jit(solution)/shard_map/reduce_scatter | solution.py:291
  1040.6 349.0 %reduce-scatter.19.cloned.1.call-start = ((), (), s32[]{:S(2)}) async-start(), calls=%async_computation.18 | async-start | bytes 7077888 | tf_op jit(solution)/shard_map/reduce_scatter | solution.py:308
  1056.9 482.5 %reduce-scatter.23.cloned.1.call-start = ((), (), s32[]{:S(2)}) async-start(), calls=%async_computation.21 | async-start | bytes 25952256 | tf_op jit(solution)/shard_map/reduce_scatter | solution.py:314
  1097.1 568.6 %all-reduce.5.cloned.1.call-start = ((), (), s32[]{:S(2)}) async-start(), calls=%async_computation.20 | async-start | bytes 131072 | tf_op jit(solution)/shard_map/psum | solution.py:303
  1112.1 211.2 %copy-start.11 = (bf16[256,2048]{1,0:T(8,128)(2,1)S(1)}, bf16[256,2048]{1,0:T(8,128)(2,1)}, u32[]{:S(2)}) copy-start(bf16[256,2048]{1,0:T(8,128)(2,1)} %param.27) | copy-start | bytes 3145732
  1112.1 211.2 %copy-start.127 = (f32[2048]{0:T(1024)S(1)}, f32[2048]{0:T(1024)}, u32[]{:S(2)}) copy-start(f32[2048]{0:T(1024)} %copy-done.126) | copy-start | bytes 24580
  1112.1 211.2 %copy-start.157 = (f32[256]{0:T(256)S(1)}, f32[256]{0:T(256)}, u32[]{:S(2)}) copy-start(f32[256]{0:T(256)} %copy-done.156) | copy-start | bytes 3076
  1112.1 213.2 %copy-start.152 = (f32[2048]{0:T(1024)S(1)}, f32[2048]{0:T(1024)}, u32[]{:S(2)}) copy-start(f32[2048]{0:T(1024)} %get-tuple-element.116) | copy-start | bytes 24580
  (184 other events, 2078.9 us)
Sparse Core Ops, SparseCore 0:
  12.8 82.8 all-gather.4
  139.4 142.8 reduce-scatter.10
  288.5 81.6 all-gather.6
  372.2 79.2 all-gather.8
  646.7 142.8 reduce-scatter.14
  792.2 77.6 reduce-scatter.12
  875.9 81.2 all-gather.10
  961.0 57.5 reduce-scatter.28
  1022.1 86.7 reduce-scatter.24
  1112.2 86.7 reduce-scatter.26
  1202.4 41.2 reduce-scatter.20
  1246.4 76.8 reduce-scatter.16
  1326.7 62.8 reduce-scatter.18
  1393.4 145.9 reduce-scatter.22
  1546.3 119.2 all-reduce.4
where the time goes:
time: 1680 us; the launch traced here: 1670 us
  waiting for transfers between devices  922 us (55%)
  matrix products  451 us (27%)
  local copies, waits for them, and re-layouts  148 us (9%)
  other arithmetic  92.2 us (5%)
  blocking collectives  42.1 us (3%)
  between operations  17.1 us (1%)
    reduce_scatter x1, waiting for transfers between devices, on_device(): lax.psum_scatter(expert_in_grad.astype(jnp.bfloat16), 'dp', scatter_dimen...  147 us
    reduce_scatter x1, waiting for transfers between devices, on_device(): lax.psum_scatter(jnp.dot(mixed, out_weight, preferred_element_type=jnp.fl...  142 us
    psum x1, waiting for transfers between devices, on_device(): lax.psum((norm_one_part, norm_two_part, router_part, gate_part, bias_full...  121 us
    reduce_scatter x1, waiting for transfers between devices, on_device(): lax.psum_scatter(shared_in_grad.astype(jnp.bfloat16), 'dp', scatter_dimen...  86.9 us
    dot_general x9, matrix products, expert_backward(): jnp.einsum('nc,dc->nd', d_gate_up, in_flat, preferred_element_type=jnp.fl...  83.9 us
    dot_general x9, matrix products, expert_forward(): result = jnp.dot(inner_act, down_weight, preferred_element_type=jnp.float32)  79.8 us
    reduce_scatter x1, waiting for transfers between devices, on_device(): lax.psum_scatter(grad_one.astype(jnp.bfloat16), 'tensor', scatter_dimensi...  77.9 us
    reduce_scatter x1, waiting for transfers between devices, on_device(): lax.psum_scatter(combined.astype(jnp.bfloat16), 'tensor', scatter_dimensi...  77 us
  transfers between devices with their start and end apart: 15, of which 14 were waited for; matrix products, arithmetic and copies ran while one was open for 25% of the time, Pallas kernels for 0%

commit v1 on v0

--- a/solution.py
+++ b/solution.py
@@ -103,9 +103,15 @@
     gain_two = norm_two.astype(jnp.float32)
     inv_one = lax.rsqrt(jnp.mean(tokens_f * tokens_f, axis=-1, keepdims=True) + epsilon)
     unit_one = tokens_f * inv_one
-    normed_one = lax.all_gather(
-        (unit_one * gain_one).astype(jnp.bfloat16), "tensor", axis=0, tiled=True
-    )
+    shard = (unit_one * gain_one).astype(jnp.bfloat16)
+    ways = lax.axis_size("tensor")
+    pieces = [shard]
+    for far in range(1, ways):
+        pieces.append(
+            lax.ppermute(pieces[far - 1], "tensor", [(d, (d - 1) % ways) for d in range(ways)])
+        )
+    line = jnp.concatenate(pieces, axis=0)
+    normed_one = jnp.roll(line, lax.axis_index("tensor") * shard.shape[0], axis=0)
     qkv_flat_weight = qkv_weight.reshape(model_width, 3 * qkv_cols)
     qkv_all = jnp.dot(normed_one, qkv_flat_weight, preferred_element_type=jnp.float32)
     qkv_all = qkv_all.reshape(slot_count, 3, qkv_cols) + qkv_bias.astype(jnp.float32)

time: 1680 us -> 1670 us (level)
  waiting for transfers between devices: 922 us -> 871 us
    reduce_scatter x1, waiting for transfers between devices: 86.9 us -> 4.11 us  [on_device(): lax.psum_scatter(shared_in_grad.astype(jnp.bfloat16), 'dp', scatter_dimen...]
    reduce_scatter x1, waiting for transfers between devices: 4.1 us -> 85.9 us  [on_device(): lax.psum_scatter(expert_out_grad.astype(jnp.bfloat16), 'dp', scatter_dime...]
    all_gather x1 -> x0, waiting for transfers between devices: 69.4 us -> none  [on_device(): lax.all_gather((unit_one * gain_one).astype(jnp.bfloat16), 'tensor', axis...]
    ppermute x0 -> x3, waiting for transfers between devices: none -> 45 us  [on_device(): lax.ppermute(pieces[far - 1], 'tensor', [(d, (d - 1) % ways) for d in ran...]
    all_gather x1, waiting for transfers between devices: 34.5 us -> 1.95 us  [on_device(): lax.all_gather((live_own * grad_out).astype(jnp.bfloat16), 'tensor', axis...]
  transfers between devices with their start and end apart: 15 -> 17, of which waited for: 14 -> 16; matrix products, arithmetic and copies ran while one was open for 25% -> 28% of each run, Pallas kernels for 0% -> 0%
where the time goes in v1:
time: 1670 us; the launch traced here: 1660 us
  waiting for transfers between devices  871 us (52%)
  matrix products  467 us (28%)
  local copies, waits for them, and re-layouts  157 us (9%)
  other arithmetic  95.2 us (6%)
  blocking collectives  42.1 us (3%)
  between operations  17 us (1%)
    reduce_scatter x1, waiting for transfers between devices, on_device(): lax.psum_scatter(jnp.dot(mixed, out_weight, preferred_element_type=jnp.fl...  148 us
    reduce_scatter x1, waiting for transfers between devices, on_device(): lax.psum_scatter(expert_in_grad.astype(jnp.bfloat16), 'dp', scatter_dimen...  148 us
    psum x1, waiting for transfers between devices, on_device(): lax.psum((norm_one_part, norm_two_part, router_part, gate_part, bias_full...  121 us
    reduce_scatter x1, waiting for transfers between devices, on_device(): lax.psum_scatter(expert_out_grad.astype(jnp.bfloat16), 'dp', scatter_dime...  85.9 us
    dot_general x9, matrix products, expert_backward(): jnp.einsum('nc,dc->nd', d_gate_up, in_flat, preferred_element_type=jnp.fl...  84.8 us
    dot_general x9, matrix products, expert_forward(): result = jnp.dot(inner_act, down_weight, preferred_element_type=jnp.float32)  79.7 us
    reduce_scatter x1, waiting for transfers between devices, on_device(): lax.psum_scatter(grad_one.astype(jnp.bfloat16), 'tensor', scatter_dimensi...  78 us
    reduce_scatter x1, waiting for transfers between devices, on_device(): lax.psum_scatter(combined.astype(jnp.bfloat16), 'tensor', scatter_dimensi...  77 us
  transfers between devices with their start and end apart: 17, of which 16 were waited for; matrix products, arithmetic and copies ran while one was open for 28% of the time, Pallas kernels for 0%

profile of v1, /device:TPU:1, one launch (start us, length us, event | category | flops | bytes accessed | tf_op | source)
XLA Modules:
  0.0 1663.6 jit_solution(12349352668050396719)
XLA Ops:
  17.2 21.8 %collective-permute-done = bf16[256,2048]{1,0:T(8,128)(2,1)} collective-permute-done((bf16[256,2048]{1,0:T(8,128)(2,1)S(1)}, bf16[256,2048]{1,0:T(8,128)(2,1)}, u32[]{:S(2)}, u32[]{:S(2)}) %collective-permute-start) | collective-permute-done | bytes 1048608 | tf_op jit(solution)/shard_map/ppermute | solution.py:111
  74.7 14.0 collective-permute-done.2
  96.5 11.6 fusion.458
  142.8 148.3 %reduce-scatter.11.cloned.1.call-done = f32[256,2048]{1,0:T(8,128)} async-done(((f32[1024,2048]{1,0:T(8,128)}), f32[256,2048]{1,0:T(8,128)}) %reduce-scatter.11.cloned.1.call-update) | async-done | bytes 2097168 | tf_op jit(solution)/shard_map/reduce_scatter | solution.py:161
  298.4 11.5 copy.161
  309.9 15.1 copy.107
  325.5 16.4 fusion.452
  342.1 36.9 %all-gather.4.cloned.1.call-done = bf16[1024,2048]{1,0:T(8,128)(2,1)} async-done(((bf16[256,2048]{1,0:T(8,128)(2,1)}), bf16[1024,2048]{1,0:T(8,128)(2,1)}) %all-gather.4.cloned.1.call-update) | async-done | bytes 4194320 | tf_op jit(solution)/shard_map/all_gather | solution.py:170
  435.3 16.0 fusion.46
  584.0 14.0 multiply_bitcast_fusion.1
  598.1 38.0 %fusion.19 = f32[1024,2048]{1,0:T(8,128)} fusion(f32[1024,2048]{1,0:T(8,128)} %fusion.506, f32[1024,2048]{1,0:T(8,128)} %fusion.505, f32[1024,2048]{1,0:T(8,128)} %fusion.504, f32[1024,2048]{1,0:T(8,128)} %fusion.503, f32[1024,2048]{1,0:T(8,128)} %fusion.502, f32[1024,2048]{1,0:T(8,128)} %fusion.501, f32[1024,2048]{1,0:T(8,128)} %fusion.500, ...), kind=kOutput, calls=%fused_computation.32 | convolution fusion | flops 11837112320 | bytes 101199872 | tf_op jit(solution)/shard_map/nc,dc->nd/dot_general | solution.py:67
  686.9 29.5 %add_convert_fusion = bf16[1024,2048]{1,0:T(8,128)(2,1)} fusion(f32[1024,2048]{1,0:T(8,128)} %fusion.321, f32[1024,2048]{1,0:T(8,128)} %fusion.325, f32[1024,2048]{1,0:T(8,128)} %fusion.329, f32[1024,2048]{1,0:T(8,128)} %fusion.333, f32[1024,2048]{1,0:T(8,128)} %fusion.337, f32[1024,2048]{1,0:T(8,128)} %fusion.341, f32[1024,2048]{1,0:T(8,128)} %fusion.345, ...), kind=kOutput, calls=%fused_computation.36 | convolution fusion | flops 5943328768 | bytes 79990784 | tf_op jit(solution)/shard_map/dot_general | solution.py:54
  716.5 62.6 %reduce-scatter.15.cloned.1.call-done = f32[256,2048]{1,0:T(8,128)} async-done(((f32[1024,2048]{1,0:T(8,128)}), f32[256,2048]{1,0:T(8,128)}) %reduce-scatter.15.cloned.1.call-update) | async-done | bytes 2097168 | tf_op jit(solution)/shard_map/reduce_scatter | solution.py:235
  782.5 77.0 %reduce-scatter.13.cloned.1.call-done = bf16[256,2048]{1,0:T(8,128)(2,1)} async-done(((bf16[1024,2048]{1,0:T(8,128)(2,1)}), bf16[256,2048]{1,0:T(8,128)(2,1)}) %reduce-scatter.13.cloned.1.call-update) | async-done | bytes 1048592 | tf_op jit(solution)/shard_map/reduce_scatter | solution.py:193
  890.5 19.2 %convolution_convert_fusion = bf16[2048,2,1408]{2,0,1:T(8,128)(2,1)} fusion(bf16[1024,2,1408]{0,2,1:T(8,128)(2,1)} %copy.137, bf16[1024,2048]{1,0:T(8,128)(2,1)} %all-gather.4.cloned.1.call-done), kind=kOutput, calls=%fused_computation.12 | convolution fusion | flops 11816927232 | bytes 21495808 | tf_op jit(solution)/shard_map/nd,nc->dc/dot_general | solution.py:66
  1018.2 12.0 bitcast_convert_fusion
  1034.9 11.5 convolution_convert_fusion.2
  1102.9 85.9 %reduce-scatter.25.cloned.1.call-done = bf16[8,352,256]{2,1,0:T(8,128)(2,1)} async-done(((bf16[8,352,2048]{2,1,0:T(8,128)(2,1)}), bf16[8,352,256]{2,1,0:T(8,128)(2,1)}) %reduce-scatter.25.cloned.1.call-update) | async-done | bytes 1441808 | tf_op jit(solution)/shard_map/reduce_scatter | solution.py:323
  1192.0 41.2 %reduce-scatter.21.cloned.1.call-done = bf16[512,256]{1,0:T(8,128)(2,1)} async-done(((bf16[512,2048]{1,0:T(8,128)(2,1)}), bf16[512,256]{1,0:T(8,128)(2,1)}) %reduce-scatter.21.cloned.1.call-update) | async-done | bytes 262160 | tf_op jit(solution)/shard_map/reduce_scatter | solution.py:317
  1235.0 78.0 %reduce-scatter.17.cloned.1.call-done = bf16[256,2048]{1,0:T(8,128)(2,1)} async-done(((bf16[1024,2048]{1,0:T(8,128)(2,1)}), bf16[256,2048]{1,0:T(8,128)(2,1)}) %reduce-scatter.17.cloned.1.call-update) | async-done | bytes 1048592 | tf_op jit(solution)/shard_map/reduce_scatter | solution.py:297
  1315.1 42.1 %all-reduce.2 = (f32[2048]{0:T(1024)}, f32[3,2048]{1,0:T(4,128)S(1)}, f32[2048]{0:T(1024)}, f32[2048]{0:T(1024)}) all-reduce(f32[2048]{0:T(1024)S(1)} %get-tuple-element.118, f32[3,2048]{1,0:T(4,128)S(1)} %constant_dynamic-update-slice_fusion.8, f32[2048]{0:T(1024)S(1)} %copy-done.152, ...), channel_id=1, replica_groups=mesh['dp'=8,'tensor'=4] {'dp','tensor'}, use_global_device_ids=true, to_apply=%region_28.29 | all-reduce | flops 12288 | bytes 98304 | tf_op jit(solution)/shard_map/psum | solution.py:309
  1361.6 17.5 %reduce-scatter.19.cloned.1.call-done = bf16[256,3,512]{2,0,1:T(8,128)(2,1)} async-done(((bf16[2048,3,512]{2,0,1:T(8,128)(2,1)}), bf16[256,3,512]{2,0,1:T(8,128)(2,1)}) %reduce-scatter.19.cloned.1.call-update) | async-done | bytes 786448 | tf_op jit(solution)/shard_map/reduce_scatter | solution.py:314
  1381.6 147.5 %reduce-scatter.23.cloned.1.call-done = bf16[8,256,2,352]{1,3,2,0:T(8,128)(2,1)} async-done(((bf16[8,2048,2,352]{1,3,2,0:T(8,128)(2,1)}), bf16[8,256,2,352]{1,3,2,0:T(8,128)(2,1)}) %reduce-scatter.23.cloned.1.call-update) | async-done | bytes 2883600 | tf_op jit(solution)/shard_map/reduce_scatter | solution.py:320
  1534.1 121.3 %all-reduce.5.cloned.1.call-done = f32[2048,8]{0,1:T(8,128)} async-done(((f32[2048,8]{0,1:T(8,128)}), f32[2048,8]{0,1:T(8,128)}) %all-reduce.5.cloned.1.call-update) | async-done | bytes 65552 | tf_op jit(solution)/shard_map/psum | solution.py:309
  (608 shorter events, 557.6 us)
Async XLA Ops:
  7.2 283.9 %reduce-scatter.11.cloned.1.call-start = ((), (), s32[]{:S(2)}) async-start(), calls=%async_computation.10 | async-start | bytes 10485760 | tf_op jit(solution)/shard_map/reduce_scatter | solution.py:161
  13.1 26.0 %collective-permute-start = (bf16[256,2048]{1,0:T(8,128)(2,1)S(1)}, bf16[256,2048]{1,0:T(8,128)(2,1)}, u32[]{:S(2)}, u32[]{:S(2)}) collective-permute-start(bf16[256,2048]{1,0:T(8,128)(2,1)S(1)} %get-tuple-element.133), channel_id=1, source_target_pairs={{0,3},{1,0},{2,1},{3,2},{4,7},{5,4},{6,5},{7,6},{8,11},{9,8},{10,9... | collective-permute-start | bytes 3145736 | tf_op jit(solution)/shard_map/ppermute | solution.py:111
  39.1 25.3 %collective-permute-start.1 = (bf16[256,2048]{1,0:T(8,128)(2,1)}, bf16[256,2048]{1,0:T(8,128)(2,1)}, u32[]{:S(2)}, u32[]{:S(2)}) collective-permute-start(bf16[256,2048]{1,0:T(8,128)(2,1)} %collective-permute-done), channel_id=1, source_target_pairs={{0,3},{1,0},{2,1},{3,2},{4,7},{5,4},{6,5},{7,6},{8,11},{9,8},{10,9... | collective-permute-start | bytes 3145736 | tf_op jit(solution)/shard_map/ppermute | solution.py:111
  64.4 24.3 %collective-permute-start.2 = (bf16[256,2048]{1,0:T(8,128)(2,1)}, bf16[256,2048]{1,0:T(8,128)(2,1)S(1)}, u32[]{:S(2)}, u32[]{:S(2)}) collective-permute-start(bf16[256,2048]{1,0:T(8,128)(2,1)} %collective-permute-done.1), channel_id=1, source_target_pairs={{0,3},{1,0},{2,1},{3,2},{4,7},{5,4},{6,5},{7,6},{8,11},{9,8},{10,9... | collective-permute-start | bytes 3145736 | tf_op jit(solution)/shard_map/ppermute | solution.py:111
  142.0 149.0 %copy-start.10 = (bf16[256,2048]{1,0:T(8,128)(2,1)S(1)}, bf16[256,2048]{1,0:T(8,128)(2,1)}, u32[]{:S(2)}) copy-start(bf16[256,2048]{1,0:T(8,128)(2,1)} %param.27) | copy-start | bytes 3145732
  142.1 236.9 %all-gather.4.cloned.1.call-start = ((), (), s32[]{:S(2)}) async-start(), calls=%async_computation.11 | async-start | bytes 5242880 | tf_op jit(solution)/shard_map/all_gather | solution.py:170
  142.7 151.9 %copy-start.131 = (f32[2048]{0:T(1024)}, f32[2048]{0:T(1024)S(1)}, u32[]{:S(2)}) copy-start(f32[2048]{0:T(1024)S(1)} %convert_element_type.408) | copy-start | bytes 24580
  142.7 151.8 %copy-start.164 = (f32[256]{0:T(256)}, f32[256]{0:T(256)S(1)}, u32[]{:S(2)}) copy-start(f32[256]{0:T(256)S(1)} %compare_convert_fusion) | copy-start | bytes 3076
  297.1 163.3 %all-gather.6.cloned.1.call-start = ((), (), s32[]{:S(2)}) async-start(), calls=%async_computation.13 | async-start | bytes 5242880 | tf_op jit(solution)/shard_map/all_gather | solution.py:198
  342.0 437.1 %reduce-scatter.15.cloned.1.call-start = ((), (), s32[]{:S(2)}) async-start(), calls=%async_computation.14 | async-start | bytes 10485760 | tf_op jit(solution)/shard_map/reduce_scatter | solution.py:235
  636.1 223.4 %reduce-scatter.13.cloned.1.call-start = ((), (), s32[]{:S(2)}) async-start(), calls=%async_computation.12 | async-start | bytes 5242880 | tf_op jit(solution)/shard_map/reduce_scatter | solution.py:193
  716.5 230.3 %all-gather.8.cloned.1.call-start = ((), (), s32[]{:S(2)}) async-start(), calls=%async_computation.15 | async-start | bytes 5242880 | tf_op jit(solution)/shard_map/all_gather | solution.py:238
  865.4 226.7 %reduce-scatter.29.cloned.1.call-start = ((), (), s32[]{:S(2)}) async-start(), calls=%async_computation.23 | async-start | bytes 6488064 | tf_op jit(solution)/shard_map/reduce_scatter | solution.py:329
  876.4 222.1 %reduce-scatter.27.cloned.1.call-start = ((), (), s32[]{:S(2)}) async-start(), calls=%async_computation.22 | async-start | bytes 12976128 | tf_op jit(solution)/shard_map/reduce_scatter | solution.py:326
  909.8 279.1 %reduce-scatter.25.cloned.1.call-start = ((), (), s32[]{:S(2)}) async-start(), calls=%async_computation.21 | async-start | bytes 12976128 | tf_op jit(solution)/shard_map/reduce_scatter | solution.py:323
  937.0 296.2 %reduce-scatter.21.cloned.1.call-start = ((), (), s32[]{:S(2)}) async-start(), calls=%async_computation.18 | async-start | bytes 2359296 | tf_op jit(solution)/shard_map/reduce_scatter | solution.py:317
  978.6 334.5 %reduce-scatter.17.cloned.1.call-start = ((), (), s32[]{:S(2)}) async-start(), calls=%async_computation.16 | async-start | bytes 5242880 | tf_op jit(solution)/shard_map/reduce_scatter | solution.py:297
  1030.2 348.9 %reduce-scatter.19.cloned.1.call-start = ((), (), s32[]{:S(2)}) async-start(), calls=%async_computation.17 | async-start | bytes 7077888 | tf_op jit(solution)/shard_map/reduce_scatter | solution.py:314
  1046.5 482.6 %reduce-scatter.23.cloned.1.call-start = ((), (), s32[]{:S(2)}) async-start(), calls=%async_computation.20 | async-start | bytes 25952256 | tf_op jit(solution)/shard_map/reduce_scatter | solution.py:320
  1086.7 568.7 %all-reduce.5.cloned.1.call-start = ((), (), s32[]{:S(2)}) async-start(), calls=%async_computation.19 | async-start | bytes 131072 | tf_op jit(solution)/shard_map/psum | solution.py:309
  1102.9 210.1 %copy-start.11 = (bf16[256,2048]{1,0:T(8,128)(2,1)S(1)}, bf16[256,2048]{1,0:T(8,128)(2,1)}, u32[]{:S(2)}) copy-start(bf16[256,2048]{1,0:T(8,128)(2,1)} %param.27) | copy-start | bytes 3145732
  1102.9 210.1 %copy-start.129 = (f32[2048]{0:T(1024)S(1)}, f32[2048]{0:T(1024)}, u32[]{:S(2)}) copy-start(f32[2048]{0:T(1024)} %copy-done.128) | copy-start | bytes 24580
  1102.9 210.1 %copy-start.157 = (f32[256]{0:T(256)S(1)}, f32[256]{0:T(256)}, u32[]{:S(2)}) copy-start(f32[256]{0:T(256)} %copy-done.156) | copy-start | bytes 3076
  1102.9 212.2 %copy-start.152 = (f32[2048]{0:T(1024)S(1)}, f32[2048]{0:T(1024)}, u32[]{:S(2)}) copy-start(f32[2048]{0:T(1024)} %get-tuple-element.116) | copy-start | bytes 24580
  (183 other events, 2247.1 us)
Sparse Core Ops, SparseCore 0:
  142.2 148.8 reduce-scatter.10
  297.3 81.6 all-gather.3
  381.1 79.2 all-gather.5
  636.2 142.8 reduce-scatter.14
  781.8 77.6 reduce-scatter.12
  865.5 81.2 all-gather.7
  950.6 57.5 reduce-scatter.28
  1011.7 86.7 reduce-scatter.26
  1102.0 86.7 reduce-scatter.24
  1191.9 41.2 reduce-scatter.20
  1236.2 76.7 reduce-scatter.16
  1316.2 62.8 reduce-scatter.18
  1383.2 145.9 reduce-scatter.22
  1536.1 119.2 all-reduce.4
